TPU v7x, 256 devices: a whole 4x4x8 slice. The times are simulated.
256 devices in a mesh: dp: 64 (over z_lo, y, x, core), mp: 4 (over z_hi).
Axes of the slice: x: 4, y: 4, z: 8 (z_hi: 4, z_lo: 2; z = z_hi * 2 + z_lo), core: 2. Of those that a mesh axis runs over, the one named last changes fastest.
Arguments:
- pooled_rows: float32 [8192, 1152], P('dp', 'mp'), may hold values from -8 to 8
- projection: float32 [1152, 1152], P('mp'), may hold values from -0.1875 to 0.1875
- text_rows: float32 [8192, 1152], P(('dp', 'mp')), may hold values from -8 to 8
- caption_row: int32 [8192], P('dp'), may hold values from 0 to 8191, as said below
Outputs:
- pooled_grad: float32 [8192, 1152], P('dp', 'mp')
- text_grad: float32 [8192, 1152], P(('dp', 'mp'))
Inputs may be any that keep to these rules, and one draw needn't show every extreme that they name: `caption_row`: every caption row is named by exactly one image. Of the 128 images of one index of dp, those whose caption row lies in the block of 128 rows of any one index (its own included) number 1 to 3; 3 is reached by some pair of indices.
All inputs are finite; a program needn't handle non-finite values.
Results may differ from a plain program's by a relative error of at most 0.0003.
Values sent between devices are 32-bit elements; how exact they have to be, the bound alone decides.
No kernel may reach another device: no remote copies, remote signals or barrier semaphores. Data moves between devices by JAX's collectives and lax.ppermute only.
A program may use at most 64 MiB of HBM per device.

v0:
```python
import jax
import jax.numpy as jnp
from jax import lax
from jax.sharding import PartitionSpec as P

LOGIT_SCALE = 10.0
LOGIT_BIAS = -2.0
NORM_EPS = 1e-06


def shifted(value, axis, steps):
    count = lax.axis_size(axis)
    pairs = [(source, (source + steps) % count) for source in range(count)]
    return lax.ppermute(value, axis, pairs)


def product(left, right):
    return jnp.dot(left, right, precision=lax.Precision.HIGHEST, preferred_element_type=jnp.float32)


def product_nt(left, right):
    return lax.dot_general(
        left,
        right,
        (((1,), (1,)), ((), ())),
        precision=lax.Precision.HIGHEST,
        preferred_element_type=jnp.float32,
    )


def product_tn(left, right):
    return lax.dot_general(
        left,
        right,
        (((0,), (0,)), ((), ())),
        precision=lax.Precision.HIGHEST,
        preferred_element_type=jnp.float32,
    )


def unit_rows(raw):
    scale = lax.rsqrt(jnp.sum(raw * raw, axis=1) + NORM_EPS)
    return (raw * scale[:, None], scale)


def unit_back(unit, scale, grad):
    return scale[:, None] * (grad - unit * jnp.sum(unit * grad, axis=1, keepdims=True))


def pair_terms(images, captions, image_rows, caption_rows):
    logits = LOGIT_SCALE * product_nt(images, captions) + LOGIT_BIAS
    target = image_rows[:, None] == caption_rows[None, :]
    signs = jnp.where(target, 1.0, -1.0).astype(jnp.float32)
    weights = -signs * jax.nn.sigmoid(-signs * logits)
    return (LOGIT_SCALE * product(weights, captions), LOGIT_SCALE * product_tn(weights, images))


def local(pooled_rows, projection, text_rows, caption_row):
    shards = lax.axis_size("dp")
    own_index = lax.axis_index("dp")
    column = lax.axis_index("mp")
    per_shard = pooled_rows.shape[0]
    features = pooled_rows.shape[1]
    text_count = text_rows.shape[0]
    base = per_shard // shards
    capacity = base + min(3, base - 1)
    owner = caption_row // per_shard
    target_slot = caption_row % per_shard
    onehot = (owner[:, None] == jnp.arange(shards, dtype=jnp.int32)[None, :]).astype(jnp.int32)
    before = jnp.cumsum(onehot, axis=0) - onehot
    rank = jnp.sum(before * onehot, axis=1)
    position = owner * capacity + rank
    outgoing = jnp.zeros((shards * capacity, features), jnp.float32).at[position].set(pooled_rows)
    out_slots = jnp.full((shards * capacity,), per_shard, jnp.int32).at[position].set(target_slot)
    arrived, arrived_slots = (
        lax.all_to_all(outgoing, "dp", split_axis=0, concat_axis=0, tiled=True),
        lax.all_to_all(out_slots, "dp", split_axis=0, concat_axis=0, tiled=True),
    )
    arranged = (
        jnp.zeros((per_shard, features), jnp.float32).at[arrived_slots].set(arrived, mode="drop")
    )
    projected = lax.psum(product(arranged, projection), "mp")
    images, image_scale = unit_rows(projected)
    captions, caption_scale = unit_rows(text_rows)
    image_rows = own_index * per_shard + jnp.arange(per_shard, dtype=jnp.int32)
    local_rows = column * text_count + jnp.arange(text_count, dtype=jnp.int32)
    image_zero = jnp.zeros(images.shape, jnp.float32)

    def visit(anchor, image_grad, visiting, visit_grad):
        image_term, caption_term = pair_terms(
            images, visiting, image_rows, anchor * per_shard + local_rows
        )
        return (image_grad + image_term, visit_grad + caption_term)

    def tour_step(turn, carry):
        image_grad, visiting, visit_grad = carry
        anchor = (own_index - turn) % shards
        image_grad, visit_grad = visit(anchor, image_grad, visiting, visit_grad)
        visiting, visit_grad = shifted((visiting, visit_grad), "dp", 1)
        return (image_grad, visiting, visit_grad)

    initial = (image_zero, captions, jnp.zeros(captions.shape, jnp.float32))
    image_grad, visiting, visit_grad = lax.fori_loop(0, shards - 1, tour_step, initial)
    image_grad, visit_grad = visit((own_index + 1) % shards, image_grad, visiting, visit_grad)
    caption_grad = shifted(visit_grad, "dp", 1)
    image_grad = lax.psum(image_grad, "mp")
    raw_grad = unit_back(images, image_scale, image_grad)
    column_grad = product_nt(raw_grad, projection)
    returning = jnp.take(column_grad, arrived_slots, axis=0, mode="fill", fill_value=0.0)
    came_back = lax.all_to_all(returning, "dp", split_axis=0, concat_axis=0, tiled=True)
    pooled_grad = came_back[position]
    text_grad = unit_back(captions, caption_scale, caption_grad)
    return (pooled_grad, text_grad)


def solution(mesh):
    placed = (P("dp", "mp"), P("mp", None), P(("dp", "mp"), None), P("dp"))
    return jax.shard_map(
        local,
        mesh=mesh,
        in_specs=placed,
        out_specs=(P("dp", "mp"), P(("dp", "mp"), None)),
        check_vma=False,
    )
```

profile of v0, /device:TPU:1, one launch (start us, length us, event | category | flops | bytes accessed | tf_op | source)
XLA Modules:
  0.0 848.4 jit_solution(17598125918919216452)
XLA Ops:
  10.1 10.3 %all-to-all-start = ((s32[64,3,1]{1,2,0:T(1,128)}), s32[64,3,1]{1,2,0:T(1,128)S(1)}, u32[]{:S(2)}, u32[]{:S(2)}) async-start(s32[64,3,1]{1,2,0:T(1,128)} %bitcast), calls=%async_computation | async-start | bytes 65536 | tf_op jit(solution)/shard_map/all_to_all | solution.py:77
  34.9 9.4 %all-to-all-done.1 = f32[64,3,288]{2,1,0:T(4,128)S(1)} async-done(((f32[64,3,288]{2,1,0:T(4,128)}), f32[64,3,288]{2,1,0:T(4,128)S(1)}, u32[]{:S(2)}, u32[]{:S(2)}) %all-to-all-start.1) | async-done | bytes 221216 | tf_op jit(solution)/shard_map/all_to_all | solution.py:76
  48.7 52.0 %all-reduce.3.cloned.1.call-done = f32[128,1152]{1,0:T(8,128)} async-done(((f32[128,1152]{1,0:T(8,128)}), f32[128,1152]{1,0:T(8,128)}) %all-reduce.3.cloned.1.call-update) | async-done | bytes 589840 | tf_op jit(solution)/shard_map/psum | solution.py:82
  103.7 652.1 %while.20 = (s32[]{:T(128)}, f32[128,1152]{1,0:T(8,128)S(1)}, f32[32,1152]{1,0:T(8,128)S(1)}, f32[32,1152]{1,0:T(8,128)S(1)}, s32[]{:T(128)}, /*index=5*/f32[128...) while((s32[]{:T(128)}, f32[128,1152]{1,0:T(8,128)S(1)}, ...), condition=%wide.region_9.10_spmd.clone, body=%wide.region_8.9_spmd.clone.sunk | while | flops 170426576 | bytes 4474472 | solution.py:103
  130.1 8.3 collective-permute-done.1
  151.0 8.3 collective-permute-done.1
  171.9 8.3 collective-permute-done.1
  224.2 8.3 collective-permute-done.1
  245.2 8.3 collective-permute-done.1
  266.1 8.3 collective-permute-done.1
  276.6 8.3 collective-permute-done.1
  297.5 8.3 collective-permute-done.1
  318.4 8.3 collective-permute-done.1
  339.3 8.3 collective-permute-done.1
  391.7 8.3 collective-permute-done.1
  412.6 8.3 collective-permute-done.1
  433.5 8.3 collective-permute-done.1
  444.0 8.3 collective-permute-done.1
  464.9 8.3 collective-permute-done.1
  485.8 8.3 collective-permute-done.1
  506.8 8.3 collective-permute-done.1
  559.1 8.3 collective-permute-done.1
  580.0 8.3 collective-permute-done.1
  600.9 8.3 collective-permute-done.1
  632.3 8.3 collective-permute-done.1
  674.2 8.3 collective-permute-done.1
  726.5 8.3 collective-permute-done.1
  747.4 8.3 collective-permute-done.1
  758.8 9.0 %collective-permute-done.2 = f32[32,1152]{1,0:T(8,128)S(1)} collective-permute-done((f32[32,1152]{1,0:T(8,128)S(1)}, f32[32,1152]{1,0:T(8,128)S(1)}, u32[]{:S(2)}, u32[]{:S(2)}) %collective-permute-start.2) | collective-permute-done | bytes 147488 | tf_op jit(solution)/shard_map/ppermute | solution.py:14
  768.0 46.4 %all-reduce.5.cloned.1.call-done = f32[128,1152]{1,0:T(8,128)} async-done(((f32[128,1152]{1,0:T(8,128)}), f32[128,1152]{1,0:T(8,128)}) %all-reduce.5.cloned.1.call-update) | async-done | bytes 589840 | tf_op jit(solution)/shard_map/psum | solution.py:106
  819.4 9.4 %all-to-all-start.2 = ((f32[64,3,288]{2,1,0:T(4,128)}), f32[64,3,288]{2,1,0:T(4,128)S(1)}, u32[]{:S(2)}, u32[]{:S(2)}) async-start(f32[64,3,288]{2,1,0:T(4,128)} %broadcast_select_fusion), calls=%async_computation.2 | async-start | bytes 786432 | tf_op jit(solution)/shard_map/all_to_all | solution.py:110
  829.6 10.1 %all-to-all-done.2 = f32[64,3,288]{2,1,0:T(4,128)S(1)} async-done(((f32[64,3,288]{2,1,0:T(4,128)}), f32[64,3,288]{2,1,0:T(4,128)S(1)}, u32[]{:S(2)}, u32[]{:S(2)}) %all-to-all-start.2) | async-done | bytes 221216 | tf_op jit(solution)/shard_map/all_to_all | solution.py:110
  (684 shorter events, 483.0 us)
Async XLA Ops:
  10.1 18.1 %all-to-all-start = ((s32[64,3,1]{1,2,0:T(1,128)}), s32[64,3,1]{1,2,0:T(1,128)S(1)}, u32[]{:S(2)}, u32[]{:S(2)}) async-start(s32[64,3,1]{1,2,0:T(1,128)} %bitcast), calls=%async_computation | async-start | bytes 65536 | tf_op jit(solution)/shard_map/all_to_all | solution.py:77
  28.3 16.1 %all-to-all-start.1 = ((f32[64,3,288]{2,1,0:T(4,128)}), f32[64,3,288]{2,1,0:T(4,128)S(1)}, u32[]{:S(2)}, u32[]{:S(2)}) async-start(f32[64,3,288]{2,1,0:T(4,128)} %all_to_all.28), calls=%async_computation.1 | async-start | bytes 786432 | tf_op jit(solution)/shard_map/all_to_all | solution.py:76
  33.5 67.2 %all-reduce.3.cloned.1.call-start = ((), (), s32[]{:S(2)}) async-start(), calls=%async_computation.3 | async-start | bytes 1179648 | tf_op jit(solution)/shard_map/psum | solution.py:82
  47.9 766.5 %all-reduce.5.cloned.1.call-start = ((), (), s32[]{:S(2)}) async-start(), calls=%async_computation.4 | async-start | bytes 1179648 | tf_op jit(solution)/shard_map/psum | solution.py:106
  127.9 10.4 %collective-permute-start = (f32[32,1152]{1,0:T(8,128)S(1)}, f32[32,1152]{1,0:T(8,128)S(1)}, u32[]{:S(2)}, u32[]{:S(2)}) collective-permute-start(f32[32,1152]{1,0:T(8,128)S(1)} %copy.23), channel_id=1, source_target_pairs={{0,4},{4,8},{8,12},{12,16},{16,20},{20,24},{24,28},{28,32},{32,36}... | collective-permute-start | bytes 442376 | tf_op jit(solution)/shard_map/while/body/eval_jaxpr/ppermute | solution.py:14
  169.8 10.4 %collective-permute-start = (f32[32,1152]{1,0:T(8,128)S(1)}, f32[32,1152]{1,0:T(8,128)S(1)}, u32[]{:S(2)}, u32[]{:S(2)}) collective-permute-start(f32[32,1152]{1,0:T(8,128)S(1)} %copy.23), channel_id=1, source_target_pairs={{0,4},{4,8},{8,12},{12,16},{16,20},{20,24},{24,28},{28,32},{32,36}... | collective-permute-start | bytes 442376 | tf_op jit(solution)/shard_map/while/body/eval_jaxpr/ppermute | solution.py:14
  190.7 10.4 %collective-permute-start = (f32[32,1152]{1,0:T(8,128)S(1)}, f32[32,1152]{1,0:T(8,128)S(1)}, u32[]{:S(2)}, u32[]{:S(2)}) collective-permute-start(f32[32,1152]{1,0:T(8,128)S(1)} %copy.23), channel_id=1, source_target_pairs={{0,4},{4,8},{8,12},{12,16},{16,20},{20,24},{24,28},{28,32},{32,36}... | collective-permute-start | bytes 442376 | tf_op jit(solution)/shard_map/while/body/eval_jaxpr/ppermute | solution.py:14
  211.6 10.4 %collective-permute-start = (f32[32,1152]{1,0:T(8,128)S(1)}, f32[32,1152]{1,0:T(8,128)S(1)}, u32[]{:S(2)}, u32[]{:S(2)}) collective-permute-start(f32[32,1152]{1,0:T(8,128)S(1)} %copy.23), channel_id=1, source_target_pairs={{0,4},{4,8},{8,12},{12,16},{16,20},{20,24},{24,28},{28,32},{32,36}... | collective-permute-start | bytes 442376 | tf_op jit(solution)/shard_map/while/body/eval_jaxpr/ppermute | solution.py:14
  222.1 10.4 %collective-permute-start = (f32[32,1152]{1,0:T(8,128)S(1)}, f32[32,1152]{1,0:T(8,128)S(1)}, u32[]{:S(2)}, u32[]{:S(2)}) collective-permute-start(f32[32,1152]{1,0:T(8,128)S(1)} %copy.23), channel_id=1, source_target_pairs={{0,4},{4,8},{8,12},{12,16},{16,20},{20,24},{24,28},{28,32},{32,36}... | collective-permute-start | bytes 442376 | tf_op jit(solution)/shard_map/while/body/eval_jaxpr/ppermute | solution.py:14
  243.0 10.4 %collective-permute-start = (f32[32,1152]{1,0:T(8,128)S(1)}, f32[32,1152]{1,0:T(8,128)S(1)}, u32[]{:S(2)}, u32[]{:S(2)}) collective-permute-start(f32[32,1152]{1,0:T(8,128)S(1)} %copy.23), channel_id=1, source_target_pairs={{0,4},{4,8},{8,12},{12,16},{16,20},{20,24},{24,28},{28,32},{32,36}... | collective-permute-start | bytes 442376 | tf_op jit(solution)/shard_map/while/body/eval_jaxpr/ppermute | solution.py:14
  263.9 10.4 %collective-permute-start = (f32[32,1152]{1,0:T(8,128)S(1)}, f32[32,1152]{1,0:T(8,128)S(1)}, u32[]{:S(2)}, u32[]{:S(2)}) collective-permute-start(f32[32,1152]{1,0:T(8,128)S(1)} %copy.23), channel_id=1, source_target_pairs={{0,4},{4,8},{8,12},{12,16},{16,20},{20,24},{24,28},{28,32},{32,36}... | collective-permute-start | bytes 442376 | tf_op jit(solution)/shard_map/while/body/eval_jaxpr/ppermute | solution.py:14
  295.3 10.4 %collective-permute-start = (f32[32,1152]{1,0:T(8,128)S(1)}, f32[32,1152]{1,0:T(8,128)S(1)}, u32[]{:S(2)}, u32[]{:S(2)}) collective-permute-start(f32[32,1152]{1,0:T(8,128)S(1)} %copy.23), channel_id=1, source_target_pairs={{0,4},{4,8},{8,12},{12,16},{16,20},{20,24},{24,28},{28,32},{32,36}... | collective-permute-start | bytes 442376 | tf_op jit(solution)/shard_map/while/body/eval_jaxpr/ppermute | solution.py:14
  337.2 10.4 %collective-permute-start = (f32[32,1152]{1,0:T(8,128)S(1)}, f32[32,1152]{1,0:T(8,128)S(1)}, u32[]{:S(2)}, u32[]{:S(2)}) collective-permute-start(f32[32,1152]{1,0:T(8,128)S(1)} %copy.23), channel_id=1, source_target_pairs={{0,4},{4,8},{8,12},{12,16},{16,20},{20,24},{24,28},{28,32},{32,36}... | collective-permute-start | bytes 442376 | tf_op jit(solution)/shard_map/while/body/eval_jaxpr/ppermute | solution.py:14
  358.1 10.4 %collective-permute-start = (f32[32,1152]{1,0:T(8,128)S(1)}, f32[32,1152]{1,0:T(8,128)S(1)}, u32[]{:S(2)}, u32[]{:S(2)}) collective-permute-start(f32[32,1152]{1,0:T(8,128)S(1)} %copy.23), channel_id=1, source_target_pairs={{0,4},{4,8},{8,12},{12,16},{16,20},{20,24},{24,28},{28,32},{32,36}... | collective-permute-start | bytes 442376 | tf_op jit(solution)/shard_map/while/body/eval_jaxpr/ppermute | solution.py:14
  379.0 10.4 %collective-permute-start = (f32[32,1152]{1,0:T(8,128)S(1)}, f32[32,1152]{1,0:T(8,128)S(1)}, u32[]{:S(2)}, u32[]{:S(2)}) collective-permute-start(f32[32,1152]{1,0:T(8,128)S(1)} %copy.23), channel_id=1, source_target_pairs={{0,4},{4,8},{8,12},{12,16},{16,20},{20,24},{24,28},{28,32},{32,36}... | collective-permute-start | bytes 442376 | tf_op jit(solution)/shard_map/while/body/eval_jaxpr/ppermute | solution.py:14
  389.5 10.4 %collective-permute-start = (f32[32,1152]{1,0:T(8,128)S(1)}, f32[32,1152]{1,0:T(8,128)S(1)}, u32[]{:S(2)}, u32[]{:S(2)}) collective-permute-start(f32[32,1152]{1,0:T(8,128)S(1)} %copy.23), channel_id=1, source_target_pairs={{0,4},{4,8},{8,12},{12,16},{16,20},{20,24},{24,28},{28,32},{32,36}... | collective-permute-start | bytes 442376 | tf_op jit(solution)/shard_map/while/body/eval_jaxpr/ppermute | solution.py:14
  410.4 10.4 %collective-permute-start = (f32[32,1152]{1,0:T(8,128)S(1)}, f32[32,1152]{1,0:T(8,128)S(1)}, u32[]{:S(2)}, u32[]{:S(2)}) collective-permute-start(f32[32,1152]{1,0:T(8,128)S(1)} %copy.23), channel_id=1, source_target_pairs={{0,4},{4,8},{8,12},{12,16},{16,20},{20,24},{24,28},{28,32},{32,36}... | collective-permute-start | bytes 442376 | tf_op jit(solution)/shard_map/while/body/eval_jaxpr/ppermute | solution.py:14
  431.4 10.4 %collective-permute-start = (f32[32,1152]{1,0:T(8,128)S(1)}, f32[32,1152]{1,0:T(8,128)S(1)}, u32[]{:S(2)}, u32[]{:S(2)}) collective-permute-start(f32[32,1152]{1,0:T(8,128)S(1)} %copy.23), channel_id=1, source_target_pairs={{0,4},{4,8},{8,12},{12,16},{16,20},{20,24},{24,28},{28,32},{32,36}... | collective-permute-start | bytes 442376 | tf_op jit(solution)/shard_map/while/body/eval_jaxpr/ppermute | solution.py:14
  462.8 10.4 %collective-permute-start = (f32[32,1152]{1,0:T(8,128)S(1)}, f32[32,1152]{1,0:T(8,128)S(1)}, u32[]{:S(2)}, u32[]{:S(2)}) collective-permute-start(f32[32,1152]{1,0:T(8,128)S(1)} %copy.23), channel_id=1, source_target_pairs={{0,4},{4,8},{8,12},{12,16},{16,20},{20,24},{24,28},{28,32},{32,36}... | collective-permute-start | bytes 442376 | tf_op jit(solution)/shard_map/while/body/eval_jaxpr/ppermute | solution.py:14
  504.6 10.4 %collective-permute-start = (f32[32,1152]{1,0:T(8,128)S(1)}, f32[32,1152]{1,0:T(8,128)S(1)}, u32[]{:S(2)}, u32[]{:S(2)}) collective-permute-start(f32[32,1152]{1,0:T(8,128)S(1)} %copy.23), channel_id=1, source_target_pairs={{0,4},{4,8},{8,12},{12,16},{16,20},{20,24},{24,28},{28,32},{32,36}... | collective-permute-start | bytes 442376 | tf_op jit(solution)/shard_map/while/body/eval_jaxpr/ppermute | solution.py:14
  525.5 10.4 %collective-permute-start = (f32[32,1152]{1,0:T(8,128)S(1)}, f32[32,1152]{1,0:T(8,128)S(1)}, u32[]{:S(2)}, u32[]{:S(2)}) collective-permute-start(f32[32,1152]{1,0:T(8,128)S(1)} %copy.23), channel_id=1, source_target_pairs={{0,4},{4,8},{8,12},{12,16},{16,20},{20,24},{24,28},{28,32},{32,36}... | collective-permute-start | bytes 442376 | tf_op jit(solution)/shard_map/while/body/eval_jaxpr/ppermute | solution.py:14
  546.5 10.4 %collective-permute-start = (f32[32,1152]{1,0:T(8,128)S(1)}, f32[32,1152]{1,0:T(8,128)S(1)}, u32[]{:S(2)}, u32[]{:S(2)}) collective-permute-start(f32[32,1152]{1,0:T(8,128)S(1)} %copy.23), channel_id=1, source_target_pairs={{0,4},{4,8},{8,12},{12,16},{16,20},{20,24},{24,28},{28,32},{32,36}... | collective-permute-start | bytes 442376 | tf_op jit(solution)/shard_map/while/body/eval_jaxpr/ppermute | solution.py:14
  556.9 10.4 %collective-permute-start = (f32[32,1152]{1,0:T(8,128)S(1)}, f32[32,1152]{1,0:T(8,128)S(1)}, u32[]{:S(2)}, u32[]{:S(2)}) collective-permute-start(f32[32,1152]{1,0:T(8,128)S(1)} %copy.23), channel_id=1, source_target_pairs={{0,4},{4,8},{8,12},{12,16},{16,20},{20,24},{24,28},{28,32},{32,36}... | collective-permute-start | bytes 442376 | tf_op jit(solution)/shard_map/while/body/eval_jaxpr/ppermute | solution.py:14
  577.9 10.4 %collective-permute-start = (f32[32,1152]{1,0:T(8,128)S(1)}, f32[32,1152]{1,0:T(8,128)S(1)}, u32[]{:S(2)}, u32[]{:S(2)}) collective-permute-start(f32[32,1152]{1,0:T(8,128)S(1)} %copy.23), channel_id=1, source_target_pairs={{0,4},{4,8},{8,12},{12,16},{16,20},{20,24},{24,28},{28,32},{32,36}... | collective-permute-start | bytes 442376 | tf_op jit(solution)/shard_map/while/body/eval_jaxpr/ppermute | solution.py:14
  598.8 10.4 %collective-permute-start = (f32[32,1152]{1,0:T(8,128)S(1)}, f32[32,1152]{1,0:T(8,128)S(1)}, u32[]{:S(2)}, u32[]{:S(2)}) collective-permute-start(f32[32,1152]{1,0:T(8,128)S(1)} %copy.23), channel_id=1, source_target_pairs={{0,4},{4,8},{8,12},{12,16},{16,20},{20,24},{24,28},{28,32},{32,36}... | collective-permute-start | bytes 442376 | tf_op jit(solution)/shard_map/while/body/eval_jaxpr/ppermute | solution.py:14
  630.2 10.4 %collective-permute-start = (f32[32,1152]{1,0:T(8,128)S(1)}, f32[32,1152]{1,0:T(8,128)S(1)}, u32[]{:S(2)}, u32[]{:S(2)}) collective-permute-start(f32[32,1152]{1,0:T(8,128)S(1)} %copy.23), channel_id=1, source_target_pairs={{0,4},{4,8},{8,12},{12,16},{16,20},{20,24},{24,28},{28,32},{32,36}... | collective-permute-start | bytes 442376 | tf_op jit(solution)/shard_map/while/body/eval_jaxpr/ppermute | solution.py:14
  672.0 10.4 %collective-permute-start = (f32[32,1152]{1,0:T(8,128)S(1)}, f32[32,1152]{1,0:T(8,128)S(1)}, u32[]{:S(2)}, u32[]{:S(2)}) collective-permute-start(f32[32,1152]{1,0:T(8,128)S(1)} %copy.23), channel_id=1, source_target_pairs={{0,4},{4,8},{8,12},{12,16},{16,20},{20,24},{24,28},{28,32},{32,36}... | collective-permute-start | bytes 442376 | tf_op jit(solution)/shard_map/while/body/eval_jaxpr/ppermute | solution.py:14
  693.0 10.4 %collective-permute-start = (f32[32,1152]{1,0:T(8,128)S(1)}, f32[32,1152]{1,0:T(8,128)S(1)}, u32[]{:S(2)}, u32[]{:S(2)}) collective-permute-start(f32[32,1152]{1,0:T(8,128)S(1)} %copy.23), channel_id=1, source_target_pairs={{0,4},{4,8},{8,12},{12,16},{16,20},{20,24},{24,28},{28,32},{32,36}... | collective-permute-start | bytes 442376 | tf_op jit(solution)/shard_map/while/body/eval_jaxpr/ppermute | solution.py:14
  713.9 10.4 %collective-permute-start = (f32[32,1152]{1,0:T(8,128)S(1)}, f32[32,1152]{1,0:T(8,128)S(1)}, u32[]{:S(2)}, u32[]{:S(2)}) collective-permute-start(f32[32,1152]{1,0:T(8,128)S(1)} %copy.23), channel_id=1, source_target_pairs={{0,4},{4,8},{8,12},{12,16},{16,20},{20,24},{24,28},{28,32},{32,36}... | collective-permute-start | bytes 442376 | tf_op jit(solution)/shard_map/while/body/eval_jaxpr/ppermute | solution.py:14
  724.3 10.4 %collective-permute-start = (f32[32,1152]{1,0:T(8,128)S(1)}, f32[32,1152]{1,0:T(8,128)S(1)}, u32[]{:S(2)}, u32[]{:S(2)}) collective-permute-start(f32[32,1152]{1,0:T(8,128)S(1)} %copy.23), channel_id=1, source_target_pairs={{0,4},{4,8},{8,12},{12,16},{16,20},{20,24},{24,28},{28,32},{32,36}... | collective-permute-start | bytes 442376 | tf_op jit(solution)/shard_map/while/body/eval_jaxpr/ppermute | solution.py:14
  745.3 10.4 %collective-permute-start = (f32[32,1152]{1,0:T(8,128)S(1)}, f32[32,1152]{1,0:T(8,128)S(1)}, u32[]{:S(2)}, u32[]{:S(2)}) collective-permute-start(f32[32,1152]{1,0:T(8,128)S(1)} %copy.23), channel_id=1, source_target_pairs={{0,4},{4,8},{8,12},{12,16},{16,20},{20,24},{24,28},{28,32},{32,36}... | collective-permute-start | bytes 442376 | tf_op jit(solution)/shard_map/while/body/eval_jaxpr/ppermute | solution.py:14
  819.4 20.3 %all-to-all-start.2 = ((f32[64,3,288]{2,1,0:T(4,128)}), f32[64,3,288]{2,1,0:T(4,128)S(1)}, u32[]{:S(2)}, u32[]{:S(2)}) async-start(f32[64,3,288]{2,1,0:T(4,128)} %broadcast_select_fusion), calls=%async_computation.2 | async-start | bytes 786432 | tf_op jit(solution)/shard_map/all_to_all | solution.py:110
  (114 other events, 1217.5 us)
Sparse Core Ops, SparseCore 0:
  48.0 52.5 all-reduce.2
  758.1 56.2 all-reduce.4
where the time goes:
time: 849 us; the launch traced here: 848 us
  waiting for transfers between devices  641 us (76%)
  matrix products  126 us (15%)
  starting transfers between devices  41.3 us (5%)
  between operations  14.4 us (2%)
  local copies, waits for them, and re-layouts  10.9 us (1%)
  other arithmetic  9.73 us (1%)
    ppermute x127, waiting for transfers between devices, shifted(): return lax.ppermute(value, axis, pairs)  519 us
    dot_general x65, matrix products, product(): jnp.dot(left, right, precision=lax.Precision.HIGHEST, preferred_element_t...  52.2 us
    psum x1, waiting for transfers between devices, local(): projected = lax.psum(product(arranged, projection), 'mp')  52 us
    psum x1, waiting for transfers between devices, local(): image_grad = lax.psum(image_grad, 'mp')  46.4 us
    dot_general x65, matrix products, product_nt(): lax.dot_general(left, right, (((1,), (1,)), ((), ())), precision=lax.Prec...  46.4 us
    dot_general x64, matrix products, product_tn(): lax.dot_general(left, right, (((0,), (0,)), ((), ())), precision=lax.Prec...  27.3 us
  transfers between devices with their start and end apart: 132, of which 69 were waited for; matrix products, arithmetic and copies ran while one was open for 15% of the time, Pallas kernels for 0%

commit v1 on v0

--- a/solution.py
+++ b/solution.py
@@ -79,7 +79,7 @@
     arranged = (
         jnp.zeros((per_shard, features), jnp.float32).at[arrived_slots].set(arrived, mode="drop")
     )
-    projected = lax.psum(product(arranged, projection), "mp")
+    projected = jnp.sum(lax.all_gather(product(arranged, projection), "mp"), axis=0)
     images, image_scale = unit_rows(projected)
     captions, caption_scale = unit_rows(text_rows)
     image_rows = own_index * per_shard + jnp.arange(per_shard, dtype=jnp.int32)

time: 849 us -> 953 us (1.12)
  matrix products: 126 us -> 209 us
  other arithmetic: 9.73 us -> 41.8 us
    psum x1 -> x0, waiting for transfers between devices: 52 us -> none  [local(): projected = lax.psum(product(arranged, projection), 'mp')]
    all_gather x0 -> x1, waiting for transfers between devices: none -> 51.8 us  [local(): lax.all_gather(product(arranged, projection), 'mp')]
    dot_general x64, matrix products: 27.3 us -> 69.1 us  [product_tn(): lax.dot_general(left, right, (((0,), (0,)), ((), ())), precision=lax.Prec...]
    dot_general x65, matrix products: 46.4 us -> 88.2 us  [product_nt(): lax.dot_general(left, right, (((1,), (1,)), ((), ())), precision=lax.Prec...]
    add x64, other arithmetic: 0.23 us -> 32.9 us  [local(): image_rows = own_index * per_shard + jnp.arange(per_shard, dtype=jnp.int32)]
  transfers between devices with their start and end apart: 132 -> 132, of which waited for: 69 -> 69; matrix products, arithmetic and copies ran while one was open for 15% -> 25% of each run, Pallas kernels for 0% -> 0%
where the time goes in v1:
time: 953 us; the launch traced here: 951 us
  waiting for transfers between devices  636 us (67%)
  matrix products  209 us (22%)
  other arithmetic  41.8 us (4%)
  starting transfers between devices  34.8 us (4%)
  between operations  14.3 us (2%)
  local copies, waits for them, and re-layouts  11.9 us (1%)
    ppermute x127, waiting for transfers between devices, shifted(): return lax.ppermute(value, axis, pairs)  515 us
    dot_general x65, matrix products, product_nt(): lax.dot_general(left, right, (((1,), (1,)), ((), ())), precision=lax.Prec...  88.2 us
    dot_general x64, matrix products, product_tn(): lax.dot_general(left, right, (((0,), (0,)), ((), ())), precision=lax.Prec...  69.1 us
    dot_general x65, matrix products, product(): jnp.dot(left, right, precision=lax.Precision.HIGHEST, preferred_element_t...  52.2 us
    all_gather x1, waiting for transfers between devices, local(): lax.all_gather(product(arranged, projection), 'mp')  51.8 us
    psum x1, waiting for transfers between devices, local(): image_grad = lax.psum(image_grad, 'mp')  45.3 us
    add x64, other arithmetic, local(): image_rows = own_index * per_shard + jnp.arange(per_shard, dtype=jnp.int32)  32.9 us
  transfers between devices with their start and end apart: 132, of which 69 were waited for; matrix products, arithmetic and copies ran while one was open for 25% of the time, Pallas kernels for 0%

profile of v1, /device:TPU:1, one launch (start us, length us, event | category | flops | bytes accessed | tf_op | source)
XLA Modules:
  0.0 951.4 jit_solution(5633071794038677067)
XLA Ops:
  10.1 10.3 %all-to-all-start = ((s32[64,3,1]{1,2,0:T(1,128)}), s32[64,3,1]{1,2,0:T(1,128)S(1)}, u32[]{:S(2)}, u32[]{:S(2)}) async-start(s32[64,3,1]{1,2,0:T(1,128)} %bitcast), calls=%async_computation | async-start | bytes 65536 | tf_op jit(solution)/shard_map/all_to_all | solution.py:77
  34.4 9.6 %all-to-all-done.1 = f32[64,3,288]{2,1,0:T(4,128)S(1)} async-done(((f32[64,3,288]{2,1,0:T(4,128)}), f32[64,3,288]{2,1,0:T(4,128)S(1)}, u32[]{:S(2)}, u32[]{:S(2)}) %all-to-all-start.1) | async-done | bytes 221216 | tf_op jit(solution)/shard_map/all_to_all | solution.py:76
  50.1 51.8 %all-gather.3.cloned.1.call-done = f32[512,1152]{1,0:T(8,128)} async-done(((f32[128,1152]{1,0:T(8,128)}), f32[512,1152]{1,0:T(8,128)}) %all-gather.3.cloned.1.call-update) | async-done | bytes 2359312 | tf_op jit(solution)/shard_map/all_gather | solution.py:82
  104.5 754.6 %while.20 = (s32[]{:T(128)}, f32[128,1152]{1,0:T(8,128)S(1)}, f32[32,1152]{1,0:T(8,128)S(1)}, f32[32,1152]{1,0:T(8,128)S(1)}, s32[]{:T(128)}, /*index=5*/f32[128...) while((s32[]{:T(128)}, f32[128,1152]{1,0:T(8,128)S(1)}, ...), condition=%wide.region_9.10_spmd.clone, body=%wide.region_8.9_spmd.clone.sunk | while | flops 170426576 | bytes 4474472 | solution.py:103
  137.5 8.2 collective-permute-done.1
  161.6 8.2 collective-permute-done.1
  173.7 8.2 collective-permute-done.1
  185.8 8.2 collective-permute-done.1
  197.9 8.2 collective-permute-done.1
  210.0 8.2 collective-permute-done.1
  222.1 8.2 collective-permute-done.1
  234.2 8.2 collective-permute-done.1
  246.3 8.2 collective-permute-done.1
  258.4 8.2 collective-permute-done.1
  270.5 8.2 collective-permute-done.1
  282.6 8.2 collective-permute-done.1
  294.7 8.2 collective-permute-done.1
  306.8 8.2 collective-permute-done.1
  318.9 8.2 collective-permute-done.1
  330.9 8.2 collective-permute-done.1
  343.0 8.2 collective-permute-done.1
  391.4 8.2 collective-permute-done.1
  476.1 8.2 collective-permute-done.1
  560.7 8.2 collective-permute-done.1
  621.2 8.2 collective-permute-done.1
  705.8 8.2 collective-permute-done.1
  790.5 8.2 collective-permute-done.1
  850.9 8.2 collective-permute-done.1
  862.8 8.7 collective-permute-done.2
  872.2 45.3 %all-reduce.2.cloned.1.call-done = f32[128,1152]{1,0:T(8,128)} async-done(((f32[128,1152]{1,0:T(8,128)}), f32[128,1152]{1,0:T(8,128)}) %all-reduce.2.cloned.1.call-update) | async-done | bytes 589840 | tf_op jit(solution)/shard_map/psum | solution.py:106
  922.5 9.4 all-to-all-start.2
  932.6 10.1 %all-to-all-done.2 = f32[64,3,288]{2,1,0:T(4,128)S(1)} async-done(((f32[64,3,288]{2,1,0:T(4,128)}), f32[64,3,288]{2,1,0:T(4,128)S(1)}, u32[]{:S(2)}, u32[]{:S(2)}) %all-to-all-start.2) | async-done | bytes 221216 | tf_op jit(solution)/shard_map/all_to_all | solution.py:110
  (685 shorter events, 591.8 us)
Async XLA Ops:
  10.1 18.1 %all-to-all-start = ((s32[64,3,1]{1,2,0:T(1,128)}), s32[64,3,1]{1,2,0:T(1,128)S(1)}, u32[]{:S(2)}, u32[]{:S(2)}) async-start(s32[64,3,1]{1,2,0:T(1,128)} %bitcast), calls=%async_computation | async-start | bytes 65536 | tf_op jit(solution)/shard_map/all_to_all | solution.py:77
  28.3 15.7 %all-to-all-start.1 = ((f32[64,3,288]{2,1,0:T(4,128)}), f32[64,3,288]{2,1,0:T(4,128)S(1)}, u32[]{:S(2)}, u32[]{:S(2)}) async-start(f32[64,3,288]{2,1,0:T(4,128)} %all_to_all.28), calls=%async_computation.1 | async-start | bytes 786432 | tf_op jit(solution)/shard_map/all_to_all | solution.py:76
  33.0 68.9 %all-gather.3.cloned.1.call-start = ((), (), s32[]{:S(2)}) async-start(), calls=%async_computation.4 | async-start | bytes 2949120 | tf_op jit(solution)/shard_map/all_gather | solution.py:82
  47.6 869.9 %all-reduce.2.cloned.1.call-start = ((), (), s32[]{:S(2)}) async-start(), calls=%async_computation.3 | async-start | bytes 1179648 | tf_op jit(solution)/shard_map/psum | solution.py:106
  121.5 12.1 %collective-permute-start = (f32[32,1152]{1,0:T(8,128)S(1)}, f32[32,1152]{1,0:T(8,128)S(1)}, u32[]{:S(2)}, u32[]{:S(2)}) collective-permute-start(f32[32,1152]{1,0:T(8,128)S(1)} %copy.22), channel_id=1, source_target_pairs={{0,4},{4,8},{8,12},{12,16},{16,20},{20,24},{24,28},{28,32},{32,36}... | collective-permute-start | bytes 442376 | tf_op jit(solution)/shard_map/while/body/eval_jaxpr/ppermute | solution.py:14
  133.6 12.1 %collective-permute-start = (f32[32,1152]{1,0:T(8,128)S(1)}, f32[32,1152]{1,0:T(8,128)S(1)}, u32[]{:S(2)}, u32[]{:S(2)}) collective-permute-start(f32[32,1152]{1,0:T(8,128)S(1)} %copy.22), channel_id=1, source_target_pairs={{0,4},{4,8},{8,12},{12,16},{16,20},{20,24},{24,28},{28,32},{32,36}... | collective-permute-start | bytes 442376 | tf_op jit(solution)/shard_map/while/body/eval_jaxpr/ppermute | solution.py:14
  145.7 12.1 %collective-permute-start = (f32[32,1152]{1,0:T(8,128)S(1)}, f32[32,1152]{1,0:T(8,128)S(1)}, u32[]{:S(2)}, u32[]{:S(2)}) collective-permute-start(f32[32,1152]{1,0:T(8,128)S(1)} %copy.22), channel_id=1, source_target_pairs={{0,4},{4,8},{8,12},{12,16},{16,20},{20,24},{24,28},{28,32},{32,36}... | collective-permute-start | bytes 442376 | tf_op jit(solution)/shard_map/while/body/eval_jaxpr/ppermute | solution.py:14
  157.8 12.1 %collective-permute-start = (f32[32,1152]{1,0:T(8,128)S(1)}, f32[32,1152]{1,0:T(8,128)S(1)}, u32[]{:S(2)}, u32[]{:S(2)}) collective-permute-start(f32[32,1152]{1,0:T(8,128)S(1)} %copy.22), channel_id=1, source_target_pairs={{0,4},{4,8},{8,12},{12,16},{16,20},{20,24},{24,28},{28,32},{32,36}... | collective-permute-start | bytes 442376 | tf_op jit(solution)/shard_map/while/body/eval_jaxpr/ppermute | solution.py:14
  169.9 12.1 %collective-permute-start = (f32[32,1152]{1,0:T(8,128)S(1)}, f32[32,1152]{1,0:T(8,128)S(1)}, u32[]{:S(2)}, u32[]{:S(2)}) collective-permute-start(f32[32,1152]{1,0:T(8,128)S(1)} %copy.22), channel_id=1, source_target_pairs={{0,4},{4,8},{8,12},{12,16},{16,20},{20,24},{24,28},{28,32},{32,36}... | collective-permute-start | bytes 442376 | tf_op jit(solution)/shard_map/while/body/eval_jaxpr/ppermute | solution.py:14
  182.0 12.1 %collective-permute-start = (f32[32,1152]{1,0:T(8,128)S(1)}, f32[32,1152]{1,0:T(8,128)S(1)}, u32[]{:S(2)}, u32[]{:S(2)}) collective-permute-start(f32[32,1152]{1,0:T(8,128)S(1)} %copy.22), channel_id=1, source_target_pairs={{0,4},{4,8},{8,12},{12,16},{16,20},{20,24},{24,28},{28,32},{32,36}... | collective-permute-start | bytes 442376 | tf_op jit(solution)/shard_map/while/body/eval_jaxpr/ppermute | solution.py:14
  194.1 12.1 %collective-permute-start = (f32[32,1152]{1,0:T(8,128)S(1)}, f32[32,1152]{1,0:T(8,128)S(1)}, u32[]{:S(2)}, u32[]{:S(2)}) collective-permute-start(f32[32,1152]{1,0:T(8,128)S(1)} %copy.22), channel_id=1, source_target_pairs={{0,4},{4,8},{8,12},{12,16},{16,20},{20,24},{24,28},{28,32},{32,36}... | collective-permute-start | bytes 442376 | tf_op jit(solution)/shard_map/while/body/eval_jaxpr/ppermute | solution.py:14
  206.2 12.1 %collective-permute-start = (f32[32,1152]{1,0:T(8,128)S(1)}, f32[32,1152]{1,0:T(8,128)S(1)}, u32[]{:S(2)}, u32[]{:S(2)}) collective-permute-start(f32[32,1152]{1,0:T(8,128)S(1)} %copy.22), channel_id=1, source_target_pairs={{0,4},{4,8},{8,12},{12,16},{16,20},{20,24},{24,28},{28,32},{32,36}... | collective-permute-start | bytes 442376 | tf_op jit(solution)/shard_map/while/body/eval_jaxpr/ppermute | solution.py:14
  218.3 12.1 %collective-permute-start = (f32[32,1152]{1,0:T(8,128)S(1)}, f32[32,1152]{1,0:T(8,128)S(1)}, u32[]{:S(2)}, u32[]{:S(2)}) collective-permute-start(f32[32,1152]{1,0:T(8,128)S(1)} %copy.22), channel_id=1, source_target_pairs={{0,4},{4,8},{8,12},{12,16},{16,20},{20,24},{24,28},{28,32},{32,36}... | collective-permute-start | bytes 442376 | tf_op jit(solution)/shard_map/while/body/eval_jaxpr/ppermute | solution.py:14
  230.3 12.1 %collective-permute-start = (f32[32,1152]{1,0:T(8,128)S(1)}, f32[32,1152]{1,0:T(8,128)S(1)}, u32[]{:S(2)}, u32[]{:S(2)}) collective-permute-start(f32[32,1152]{1,0:T(8,128)S(1)} %copy.22), channel_id=1, source_target_pairs={{0,4},{4,8},{8,12},{12,16},{16,20},{20,24},{24,28},{28,32},{32,36}... | collective-permute-start | bytes 442376 | tf_op jit(solution)/shard_map/while/body/eval_jaxpr/ppermute | solution.py:14
  242.4 12.1 %collective-permute-start = (f32[32,1152]{1,0:T(8,128)S(1)}, f32[32,1152]{1,0:T(8,128)S(1)}, u32[]{:S(2)}, u32[]{:S(2)}) collective-permute-start(f32[32,1152]{1,0:T(8,128)S(1)} %copy.22), channel_id=1, source_target_pairs={{0,4},{4,8},{8,12},{12,16},{16,20},{20,24},{24,28},{28,32},{32,36}... | collective-permute-start | bytes 442376 | tf_op jit(solution)/shard_map/while/body/eval_jaxpr/ppermute | solution.py:14
  254.5 12.1 %collective-permute-start = (f32[32,1152]{1,0:T(8,128)S(1)}, f32[32,1152]{1,0:T(8,128)S(1)}, u32[]{:S(2)}, u32[]{:S(2)}) collective-permute-start(f32[32,1152]{1,0:T(8,128)S(1)} %copy.22), channel_id=1, source_target_pairs={{0,4},{4,8},{8,12},{12,16},{16,20},{20,24},{24,28},{28,32},{32,36}... | collective-permute-start | bytes 442376 | tf_op jit(solution)/shard_map/while/body/eval_jaxpr/ppermute | solution.py:14
  266.6 12.1 %collective-permute-start = (f32[32,1152]{1,0:T(8,128)S(1)}, f32[32,1152]{1,0:T(8,128)S(1)}, u32[]{:S(2)}, u32[]{:S(2)}) collective-permute-start(f32[32,1152]{1,0:T(8,128)S(1)} %copy.22), channel_id=1, source_target_pairs={{0,4},{4,8},{8,12},{12,16},{16,20},{20,24},{24,28},{28,32},{32,36}... | collective-permute-start | bytes 442376 | tf_op jit(solution)/shard_map/while/body/eval_jaxpr/ppermute | solution.py:14
  278.7 12.1 %collective-permute-start = (f32[32,1152]{1,0:T(8,128)S(1)}, f32[32,1152]{1,0:T(8,128)S(1)}, u32[]{:S(2)}, u32[]{:S(2)}) collective-permute-start(f32[32,1152]{1,0:T(8,128)S(1)} %copy.22), channel_id=1, source_target_pairs={{0,4},{4,8},{8,12},{12,16},{16,20},{20,24},{24,28},{28,32},{32,36}... | collective-permute-start | bytes 442376 | tf_op jit(solution)/shard_map/while/body/eval_jaxpr/ppermute | solution.py:14
  290.8 12.1 %collective-permute-start = (f32[32,1152]{1,0:T(8,128)S(1)}, f32[32,1152]{1,0:T(8,128)S(1)}, u32[]{:S(2)}, u32[]{:S(2)}) collective-permute-start(f32[32,1152]{1,0:T(8,128)S(1)} %copy.22), channel_id=1, source_target_pairs={{0,4},{4,8},{8,12},{12,16},{16,20},{20,24},{24,28},{28,32},{32,36}... | collective-permute-start | bytes 442376 | tf_op jit(solution)/shard_map/while/body/eval_jaxpr/ppermute | solution.py:14
  302.9 12.1 %collective-permute-start = (f32[32,1152]{1,0:T(8,128)S(1)}, f32[32,1152]{1,0:T(8,128)S(1)}, u32[]{:S(2)}, u32[]{:S(2)}) collective-permute-start(f32[32,1152]{1,0:T(8,128)S(1)} %copy.22), channel_id=1, source_target_pairs={{0,4},{4,8},{8,12},{12,16},{16,20},{20,24},{24,28},{28,32},{32,36}... | collective-permute-start | bytes 442376 | tf_op jit(solution)/shard_map/while/body/eval_jaxpr/ppermute | solution.py:14
  315.0 12.1 %collective-permute-start = (f32[32,1152]{1,0:T(8,128)S(1)}, f32[32,1152]{1,0:T(8,128)S(1)}, u32[]{:S(2)}, u32[]{:S(2)}) collective-permute-start(f32[32,1152]{1,0:T(8,128)S(1)} %copy.22), channel_id=1, source_target_pairs={{0,4},{4,8},{8,12},{12,16},{16,20},{20,24},{24,28},{28,32},{32,36}... | collective-permute-start | bytes 442376 | tf_op jit(solution)/shard_map/while/body/eval_jaxpr/ppermute | solution.py:14
  327.1 12.1 %collective-permute-start = (f32[32,1152]{1,0:T(8,128)S(1)}, f32[32,1152]{1,0:T(8,128)S(1)}, u32[]{:S(2)}, u32[]{:S(2)}) collective-permute-start(f32[32,1152]{1,0:T(8,128)S(1)} %copy.22), channel_id=1, source_target_pairs={{0,4},{4,8},{8,12},{12,16},{16,20},{20,24},{24,28},{28,32},{32,36}... | collective-permute-start | bytes 442376 | tf_op jit(solution)/shard_map/while/body/eval_jaxpr/ppermute | solution.py:14
  339.2 12.1 %collective-permute-start = (f32[32,1152]{1,0:T(8,128)S(1)}, f32[32,1152]{1,0:T(8,128)S(1)}, u32[]{:S(2)}, u32[]{:S(2)}) collective-permute-start(f32[32,1152]{1,0:T(8,128)S(1)} %copy.22), channel_id=1, source_target_pairs={{0,4},{4,8},{8,12},{12,16},{16,20},{20,24},{24,28},{28,32},{32,36}... | collective-permute-start | bytes 442376 | tf_op jit(solution)/shard_map/while/body/eval_jaxpr/ppermute | solution.py:14
  351.3 12.1 %collective-permute-start = (f32[32,1152]{1,0:T(8,128)S(1)}, f32[32,1152]{1,0:T(8,128)S(1)}, u32[]{:S(2)}, u32[]{:S(2)}) collective-permute-start(f32[32,1152]{1,0:T(8,128)S(1)} %copy.22), channel_id=1, source_target_pairs={{0,4},{4,8},{8,12},{12,16},{16,20},{20,24},{24,28},{28,32},{32,36}... | collective-permute-start | bytes 442376 | tf_op jit(solution)/shard_map/while/body/eval_jaxpr/ppermute | solution.py:14
  363.4 12.1 %collective-permute-start = (f32[32,1152]{1,0:T(8,128)S(1)}, f32[32,1152]{1,0:T(8,128)S(1)}, u32[]{:S(2)}, u32[]{:S(2)}) collective-permute-start(f32[32,1152]{1,0:T(8,128)S(1)} %copy.22), channel_id=1, source_target_pairs={{0,4},{4,8},{8,12},{12,16},{16,20},{20,24},{24,28},{28,32},{32,36}... | collective-permute-start | bytes 442376 | tf_op jit(solution)/shard_map/while/body/eval_jaxpr/ppermute | solution.py:14
  375.5 12.1 %collective-permute-start = (f32[32,1152]{1,0:T(8,128)S(1)}, f32[32,1152]{1,0:T(8,128)S(1)}, u32[]{:S(2)}, u32[]{:S(2)}) collective-permute-start(f32[32,1152]{1,0:T(8,128)S(1)} %copy.22), channel_id=1, source_target_pairs={{0,4},{4,8},{8,12},{12,16},{16,20},{20,24},{24,28},{28,32},{32,36}... | collective-permute-start | bytes 442376 | tf_op jit(solution)/shard_map/while/body/eval_jaxpr/ppermute | solution.py:14
  387.5 12.1 %collective-permute-start = (f32[32,1152]{1,0:T(8,128)S(1)}, f32[32,1152]{1,0:T(8,128)S(1)}, u32[]{:S(2)}, u32[]{:S(2)}) collective-permute-start(f32[32,1152]{1,0:T(8,128)S(1)} %copy.22), channel_id=1, source_target_pairs={{0,4},{4,8},{8,12},{12,16},{16,20},{20,24},{24,28},{28,32},{32,36}... | collective-permute-start | bytes 442376 | tf_op jit(solution)/shard_map/while/body/eval_jaxpr/ppermute | solution.py:14
  411.7 12.1 %collective-permute-start = (f32[32,1152]{1,0:T(8,128)S(1)}, f32[32,1152]{1,0:T(8,128)S(1)}, u32[]{:S(2)}, u32[]{:S(2)}) collective-permute-start(f32[32,1152]{1,0:T(8,128)S(1)} %copy.22), channel_id=1, source_target_pairs={{0,4},{4,8},{8,12},{12,16},{16,20},{20,24},{24,28},{28,32},{32,36}... | collective-permute-start | bytes 442376 | tf_op jit(solution)/shard_map/while/body/eval_jaxpr/ppermute | solution.py:14
  556.8 12.1 %collective-permute-start = (f32[32,1152]{1,0:T(8,128)S(1)}, f32[32,1152]{1,0:T(8,128)S(1)}, u32[]{:S(2)}, u32[]{:S(2)}) collective-permute-start(f32[32,1152]{1,0:T(8,128)S(1)} %copy.22), channel_id=1, source_target_pairs={{0,4},{4,8},{8,12},{12,16},{16,20},{20,24},{24,28},{28,32},{32,36}... | collective-permute-start | bytes 442376 | tf_op jit(solution)/shard_map/while/body/eval_jaxpr/ppermute | solution.py:14
  641.5 12.1 %collective-permute-start = (f32[32,1152]{1,0:T(8,128)S(1)}, f32[32,1152]{1,0:T(8,128)S(1)}, u32[]{:S(2)}, u32[]{:S(2)}) collective-permute-start(f32[32,1152]{1,0:T(8,128)S(1)} %copy.22), channel_id=1, source_target_pairs={{0,4},{4,8},{8,12},{12,16},{16,20},{20,24},{24,28},{28,32},{32,36}... | collective-permute-start | bytes 442376 | tf_op jit(solution)/shard_map/while/body/eval_jaxpr/ppermute | solution.py:14
  786.6 12.1 %collective-permute-start = (f32[32,1152]{1,0:T(8,128)S(1)}, f32[32,1152]{1,0:T(8,128)S(1)}, u32[]{:S(2)}, u32[]{:S(2)}) collective-permute-start(f32[32,1152]{1,0:T(8,128)S(1)} %copy.22), channel_id=1, source_target_pairs={{0,4},{4,8},{8,12},{12,16},{16,20},{20,24},{24,28},{28,32},{32,36}... | collective-permute-start | bytes 442376 | tf_op jit(solution)/shard_map/while/body/eval_jaxpr/ppermute | solution.py:14
  922.5 20.3 %all-to-all-start.2 = ((f32[64,3,288]{2,1,0:T(4,128)}), f32[64,3,288]{2,1,0:T(4,128)S(1)}, u32[]{:S(2)}, u32[]{:S(2)}) async-start(f32[64,3,288]{2,1,0:T(4,128)} %broadcast_select_fusion), calls=%async_computation.2 | async-start | bytes 786432 | tf_op jit(solution)/shard_map/all_to_all | solution.py:110
  (114 other events, 1157.3 us)
Sparse Core Ops, SparseCore 0:
  47.7 54.0 all-gather.2
  862.2 55.2 all-reduce.1
